TPU v7x, 32 devices: a whole 2x2x4 slice. The times are simulated.
32 devices in a mesh: row: 4 (over x, core), col: 8 (over z, y).
Axes of the slice: x: 2, y: 2, z: 4, core: 2. Of those that a mesh axis runs over, the one named last changes fastest.
Arguments:
- weight: bfloat16 [8192, 16384], P('row', 'col'), may hold values from -6 to 6
- gradient: bfloat16 [8192, 16384], P('row', 'col'), may hold values from -6 to 6
- old_basis: bfloat16 [8192, 1024], P('row'), may hold values from -0.0625 to 0.0625
- new_basis: bfloat16 [8192, 1024], P('row'), may hold values from -0.0625 to 0.0625
- first_moment: float32 [1024, 16384], P(None, ('col', 'row')), may hold values from -6 to 6
- second_moment: float32 [1024, 16384], P(None, ('col', 'row')), may hold values from 0.05 to 2
Outputs:
- new_weight: bfloat16 [8192, 16384], P('row', 'col')
- update: bfloat16 [8192, 16384], P('row', 'col')
- first_new: float32 [1024, 16384], P(None, ('col', 'row'))
- second_new: float32 [1024, 16384], P(None, ('col', 'row'))
All inputs are finite; a program needn't handle non-finite values.
Results may differ from a plain program's by a relative error of at most 0.0047.
Values may be sent and summed in bfloat16 or wider, within the bound.
A program may use at most 128 MiB of HBM per device.

v0:
```python
import functools

import jax
import jax.numpy as jnp
from jax import lax
from jax.experimental import pallas as pl
from jax.experimental.pallas import tpu as pltpu
from jax.sharding import PartitionSpec as P


beta_first = 0.9
beta_second = 0.95
epsilon = 1e-08
step_rate = 0.0025

CHUNKS = 2


def low(values):
    return values.astype(jnp.bfloat16)


def wide(values):
    return values.astype(jnp.float32)


def product(left, right):
    return jnp.einsum("mr,mn->rn", left, right, preferred_element_type=jnp.float32)


def swap(values, axis, size, bit):
    return lax.ppermute(values, axis, [(k, k ^ bit) for k in range(size)])


def after(values, *earlier):
    return lax.optimization_barrier((values, earlier))[0]


def in_order(own, other, second, axis):
    return jnp.where(second == 1, jnp.stack([other, own], axis), jnp.stack([own, other], axis))


def transition_piece(rows, columns, old_basis, new_basis):
    part = old_basis.shape[1] // columns
    core_at = lax.axis_index("row") & 1
    mine = lax.dynamic_slice_in_dim(old_basis, lax.axis_index("col") * part, part, axis=1)
    term = product(mine, new_basis)
    half = part // 2
    kept = lax.dynamic_slice_in_dim(term, core_at * half, half, axis=0)
    sent = lax.dynamic_slice_in_dim(term, (1 - core_at) * half, half, axis=0)
    kept = kept + swap(sent, "row", rows, 1)
    return low(kept + wide(swap(low(kept), "row", rows, 2))), kept


def along_layers(piece, columns):
    received = []
    for hop in range(1, columns // 2):
        received.append(lax.ppermute(piece, "col", [(k, (k + 2 * hop) % columns) for k in range(columns)]))
    return received


def layers_in_order(piece, received):
    layers = 1 + len(received)
    stack = jnp.concatenate([piece, *received][::-1] * 2)
    first = (layers - 1 - lax.axis_index("col") // 2) * piece.shape[0]
    return lax.dynamic_slice_in_dim(stack, first, layers * piece.shape[0], axis=0).reshape(layers, *piece.shape)


def plain_transition(columns, old_basis, new_basis):
    part = old_basis.shape[1] // columns
    mine = lax.dynamic_slice_in_dim(old_basis, lax.axis_index("col") * part, part, axis=1)
    summed = lax.psum(product(mine, new_basis), "row")
    return lax.all_gather(low(summed), "col", axis=0, tiled=True)


def stepped(flipped, squares, first_moment, second_moment, projected):
    moved_first = product(flipped, first_moment)
    moved_second = product(squares, second_moment)
    first_new = beta_first * moved_first + (1.0 - beta_first) * projected
    second_new = beta_second * moved_second + (1.0 - beta_second) * projected * projected
    return first_new, second_new, low(first_new / (jnp.sqrt(second_new) + epsilon))


def back_kernel(width, chunks, place, basis, weight, *rest):
    directions, (new_weight, update) = rest[: 2 * chunks], rest[-2:]
    ranks = basis.shape[1] // chunks

    def put(pieces, columns):
        back = jnp.zeros((basis.shape[0], width), jnp.float32)
        for k, piece in enumerate(pieces):
            back += jnp.dot(
                basis[:, k * ranks : (k + 1) * ranks], piece[...], preferred_element_type=jnp.float32
            )
        update[:, columns] = low(back)
        new_weight[:, columns] = low(wide(weight[:, columns]) - step_rate * back)

    for core in range(2):

        @pl.when(place[1] == core)
        def _():
            put(directions[:chunks], slice(core * width, (core + 1) * width))
            put(directions[chunks:], slice((1 - core) * width, (2 - core) * width))


def back_half(place, basis, weight, mine, mate, held=()):
    depth, ranks = basis.shape
    width = mine[0].shape[1]
    tile = min(512, depth)
    whole = pl.BlockSpec(mine[0].shape, lambda i, place: (0, 0))
    block = pl.BlockSpec((tile, 2 * width), lambda i, place: (i, place[0]))
    directions = [*mine, *mate]
    return pl.pallas_call(
        functools.partial(back_kernel, width, len(mine)),
        out_shape=[jax.ShapeDtypeStruct(weight.shape, jnp.bfloat16)] * 2,
        grid_spec=pltpu.PrefetchScalarGridSpec(
            num_scalar_prefetch=1,
            grid=(depth // tile,),
            in_specs=[pl.BlockSpec((tile, ranks), lambda i, place: (i, 0)), block]
            + [whole] * len(directions)
            + [pl.BlockSpec(memory_space=pl.ANY)] * len(held),
            out_specs=[block] * 2,
        ),
        input_output_aliases={3 + len(directions) + k: k for k in range(len(held))},
        compiler_params=pltpu.CompilerParams(vmem_limit_bytes=32 << 20),
        cost_estimate=pl.CostEstimate(
            flops=4 * depth * ranks * width,
            bytes_accessed=2 * (depth * ranks + 6 * depth * width + 2 * ranks * width),
            transcendentals=0,
        ),
    )(place, basis, weight, *directions, *held)


def paired(rows, columns, weight, gradient, old_basis, new_basis, first_moment, second_moment):
    width = first_moment.shape[1]
    row = lax.axis_index("row")
    chip_at, core_at = row >> 1, row & 1
    chunk = new_basis.shape[1] // CHUNKS
    parts = [slice(k * chunk, (k + 1) * chunk) for k in range(CHUNKS)]

    def columns_of(source, chip):
        return lax.dynamic_slice_in_dim(source, chip * 2 * width, 2 * width, axis=1)

    def block(values, core):
        return lax.dynamic_slice_in_dim(values, core * width, width, axis=1)

    piece, earlier = transition_piece(rows, columns, old_basis, new_basis)
    received = along_layers(piece, columns)
    far, source = [], after(gradient, earlier)
    for part in parts:
        values = product(new_basis[:, part], columns_of(source, 1 - chip_at))
        mate = swap(low(block(values, 1 - core_at)), "row", rows, 1)
        far.append(low(block(values, core_at) + wide(mate)))
        source = after(gradient, far[-1])
    from_chip = []
    for values in far:
        from_chip.append(swap(values, "row", rows, 2))
    near, from_core = [], []
    for k, part in enumerate(parts):
        values = product(new_basis[:, part], columns_of(source, chip_at))
        near.append(block(values, core_at))
        mate = low(block(values, 1 - core_at))
        from_core.append(swap(mate, "row", rows, 1))
        if k == 0:
            along = layers_in_order(piece, after(received, mate))
            beyond = swap(along, "col", columns, 1)
            source = after(gradient, along)
    both = in_order(along, after(beyond, mate), lax.axis_index("col") & 1, 1)
    flipped = in_order(both, swap(both, "row", rows, 1), core_at, 2)
    flipped = flipped.reshape(old_basis.shape[1], new_basis.shape[1])
    squares = low(jnp.square(wide(flipped)))
    first_moment, second_moment = low(first_moment), low(second_moment)
    steps, across = [], []
    for k, part in enumerate(parts):
        projected = near[k] + wide(from_core[k]) + wide(from_chip[k])
        steps.append(stepped(flipped[:, part], squares[:, part], first_moment, second_moment, projected))
        across.append(swap(steps[k][2], "row", rows, 2))
    direction = [step[2] for step in steps]
    beside = [swap(values, "row", rows, 1) for values in direction]
    held = back_half(jnp.stack([chip_at, core_at]), new_basis, weight, direction, beside)
    first_new, second_new = (jnp.concatenate([step[k] for step in steps]) for k in range(2))
    across = after(across, held, first_new, second_new)
    beyond = [swap(values, "row", rows, 1) for values in across]
    new_weight, update = back_half(jnp.stack([1 - chip_at, core_at]), new_basis, weight, across, beyond, held)
    return (new_weight, update, first_new, second_new)


def plain(columns, weight, gradient, old_basis, new_basis, first_moment, second_moment):
    flipped = plain_transition(columns, old_basis, new_basis)
    squares = low(jnp.square(wide(flipped)))
    sums = low(product(new_basis, gradient))
    projected = wide(lax.psum_scatter(sums, "row", scatter_dimension=1, tiled=True))
    first_new, second_new, direction = stepped(
        flipped, squares, low(first_moment), low(second_moment), projected
    )
    directions = lax.all_gather(direction, "row", axis=1, tiled=True)
    back = jnp.dot(new_basis, directions, preferred_element_type=jnp.float32)
    new_weight = low(wide(weight) - step_rate * back)
    return (new_weight, low(back), first_new, second_new)


def solution(mesh):
    rows, columns = mesh.shape["row"], mesh.shape["col"]
    pairs = rows == 4 and columns % 2 == 0
    placed = (
        P("row", "col"),
        P("row", "col"),
        P("row", None),
        P("row", None),
        P(None, ("col", "row")),
        P(None, ("col", "row")),
    )
    return jax.shard_map(
        functools.partial(paired, rows, columns) if pairs else functools.partial(plain, columns),
        mesh=mesh,
        in_specs=placed,
        out_specs=(
            P("row", "col"),
            P("row", "col"),
            P(None, ("col", "row")),
            P(None, ("col", "row")),
        ),
        check_vma=False,
    )
```

profile of v0, /device:TPU:0, one launch (start us, length us, event | category | flops | bytes accessed | tf_op | source)
XLA Modules:
  0.0 122.3 jit_solution(16985850736163093379)
XLA Ops:
  0.6 3.1 %fusion.40 = f32[128,1024]{1,0:T(8,128)S(1)} fusion(bf16[2048,1024]{1,0:T(8,128)(2,1)} %basis.3, bf16[2048,1024]{1,0:T(8,128)(2,1)} %param.8, s32[]{:T(128)S(6)} %select_n.70), kind=kOutput, calls=%fused_computation.55 | convolution fusion | flops 536870912 | bytes 5242884 | tf_op jit(solution)/shard_map/mr,mn->rn/dot_general | solution.py:28
  3.8 0.6 collective-permute-start
  4.4 1.2 collective-permute-done
  5.6 5.2 %fusion.6 = f32[1024,512]{0,1:T(8,128)S(1)} fusion(bf16[2048,2048]{1,0:T(8,128)(2,1)} %param.7, s32[]{:T(128)S(6)} %select_n.73, bf16[2048,1024]{1,0:T(8,128)(2,1)} %basis.3), kind=kOutput, calls=%fused_computation.7 | convolution fusion | flops 2147483648 | bytes 8388612 | tf_op jit(solution)/shard_map/mr,mn->rn/dot_general | solution.py:28
  10.8 0.1 fusion.32
  10.9 0.4 collective-permute-start.5
  11.3 1.5 %collective-permute-done.5 = bf16[512,512]{1,0:T(8,128)(2,1)S(1)} collective-permute-done((bf16[512,512]{1,0:T(8,128)(2,1)S(1)}, bf16[512,512]{1,0:T(8,128)(2,1)S(1)}, u32[]{:S(2)}, u32[]{:S(2)}) %collective-permute-start.5) | collective-permute-done | bytes 524320 | tf_op jit(solution)/shard_map/ppermute | solution.py:32
  12.9 1.0 fusion.31
  13.8 5.2 %fusion.4 = f32[1024,512]{0,1:T(8,128)S(1)} fusion(bf16[2048,2048]{1,0:T(8,128)(2,1)} %param.7, s32[]{:T(128)S(6)} %select_n.73, bf16[2048,1024]{1,0:T(8,128)(2,1)} %basis.3), kind=kOutput, calls=%fused_computation.5 | convolution fusion | flops 2147483648 | bytes 8388612 | tf_op jit(solution)/shard_map/mr,mn->rn/dot_general | solution.py:28
  19.1 0.1 fusion.33
  19.1 0.4 collective-permute-start.6
  19.6 2.6 %collective-permute-start.1 = (bf16[64,1024]{1,0:T(8,128)(2,1)S(1)}, bf16[64,1024]{1,0:T(8,128)(2,1)}, u32[]{:S(2)}, u32[]{:S(2)}) collective-permute-start(bf16[64,1024]{1,0:T(8,128)(2,1)S(1)} %get-tuple-element.32), channel_id=1, source_target_pairs={{0,16},{8,24},{16,0},{24,8},{1,17},{9,25},{17,1},{25,9},{2,18},{10... | collective-permute-start | bytes 393224 | tf_op jit(solution)/shard_map/ppermute | solution.py:32
  22.2 4.1 %collective-permute-done.1 = bf16[64,1024]{1,0:T(8,128)(2,1)} collective-permute-done((bf16[64,1024]{1,0:T(8,128)(2,1)S(1)}, bf16[64,1024]{1,0:T(8,128)(2,1)}, u32[]{:S(2)}, u32[]{:S(2)}) %collective-permute-start.1) | collective-permute-done | bytes 131104 | tf_op jit(solution)/shard_map/ppermute | solution.py:32
  26.3 0.9 add_convert_fusion
  27.3 3.9 %collective-permute-start.4 = (bf16[64,1024]{1,0:T(8,128)(2,1)S(1)}, bf16[64,1024]{1,0:T(8,128)(2,1)S(1)}, u32[]{:S(2)}, u32[]{:S(2)}) collective-permute-start(bf16[64,1024]{1,0:T(8,128)(2,1)S(1)} %add_convert_fusion), channel_id=1, source_target_pairs={{0,6},{1,7},{2,0},{3,1},{4,2},{5,3},{6,4},{7,5},{8,14},{9,15},{10,... | collective-permute-start | bytes 393224 | tf_op jit(solution)/shard_map/ppermute | solution.py:58
  31.2 0.0 collective-permute-start.3
  31.2 1.0 collective-permute-start.2
  32.2 0.0 collective-permute-done.6
  32.2 1.0 fusion.30
  33.2 5.7 %fusion.2 = f32[1024,512]{0,1:T(8,128)S(1)} fusion(bf16[2048,2048]{1,0:T(8,128)(2,1)} %param.7, s32[]{:T(128)S(6)} %select_n.76, bf16[2048,1024]{1,0:T(8,128)(2,1)} %basis.3), kind=kOutput, calls=%fused_computation.3 | convolution fusion | flops 2147483648 | bytes 8388612 | tf_op jit(solution)/shard_map/mr,mn->rn/dot_general | solution.py:28
  38.9 0.0 copy-start
  38.9 0.9 fusion.34
  39.8 0.0 collective-permute-done.4
  39.8 2.2 %collective-permute-done.3 = bf16[64,1024]{1,0:T(8,128)(2,1)S(1)} collective-permute-done((bf16[64,1024]{1,0:T(8,128)(2,1)S(1)}, bf16[64,1024]{1,0:T(8,128)(2,1)S(1)}, u32[]{:S(2)}, u32[]{:S(2)}) %collective-permute-start.3) | collective-permute-done | bytes 131104 | tf_op jit(solution)/shard_map/ppermute | solution.py:58
  42.2 1.6 %collective-permute-start.7 = (bf16[4,64,1024]{2,1,0:T(8,128)(2,1)S(1)}, bf16[4,64,1024]{2,1,0:T(8,128)(2,1)S(1)}, u32[]{:S(2)}, u32[]{:S(2)}) collective-permute-start(bf16[4,64,1024]{2,1,0:T(8,128)(2,1)S(1)} %bitcast.50), channel_id=1, source_target_pairs={{0,1},{1,0},{2,3},{3,2},{4,5},{5,4},{6,7},{7,6},{8,9},{9,8},{10,11... | collective-permute-start | bytes 1572872 | tf_op jit(solution)/shard_map/ppermute | solution.py:32
  43.8 2.4 %fusion = f32[1024,512]{0,1:T(8,128)S(1)} fusion(bf16[2048,2048]{1,0:T(8,128)(2,1)S(1)} %bitcast.57, s32[]{:T(128)S(6)} %select_n.76, bf16[2048,1024]{1,0:T(8,128)(2,1)S(1)} %copy-done), kind=kOutput, calls=%fused_computation.1 | convolution fusion | flops 2147483648 | bytes 8388612 | tf_op jit(solution)/shard_map/mr,mn->rn/dot_general | solution.py:28
  46.2 0.0 copy-start.3
  46.2 1.0 fusion.35
  47.2 8.2 %collective-permute-done.7 = bf16[4,64,1024]{2,1,0:T(8,128)(2,1)S(1)} collective-permute-done((bf16[4,64,1024]{2,1,0:T(8,128)(2,1)S(1)}, bf16[4,64,1024]{2,1,0:T(8,128)(2,1)S(1)}, u32[]{:S(2)}, u32[]{:S(2)}) %collective-permute-start.7) | collective-permute-done | bytes 524320 | tf_op jit(solution)/shard_map/ppermute | solution.py:32
  55.4 1.1 maximum_select_fusion.1
  56.5 0.0 collective-permute-start.8
  56.5 1.5 %collective-permute-start.10 = (bf16[512,512]{1,0:T(8,128)(2,1)}, bf16[512,512]{1,0:T(8,128)(2,1)S(1)}, u32[]{:S(2)}, u32[]{:S(2)}) collective-permute-start(bf16[512,512]{1,0:T(8,128)(2,1)} %fusion.31), channel_id=1, source_target_pairs={{0,16},{8,24},{16,0},{24,8},{1,17},{9,25},{17,1},{25,9},{2,18},{10... | collective-permute-start | bytes 1572872 | tf_op jit(solution)/shard_map/ppermute | solution.py:32
  58.0 0.5 collective-permute-start.13
  58.6 0.5 collective-permute-start.12
  59.1 0.1 maximum_select_fusion.2
  59.2 0.4 collective-permute-done.8
  59.5 1.3 %copy.24 = bf16[4,2,64,1024]{3,2,1,0:T(8,128)(2,1)S(1)} copy(bf16[4,2,64,1024]{3,2,0,1:T(8,128)(2,1)} %collective-permute-done.8) | data formatting | bytes 2097152 | tf_op jit(solution)/shard_map/ppermute | solution.py:32
  60.9 0.2 maximum_select_fusion
  61.1 0.0 copy-start.2
  61.1 0.0 copy-start.4
  61.1 0.7 multiply_convert_fusion
  61.7 0.0 copy-start.5
  61.8 20.6 %collective-permute-done.13 = bf16[512,512]{1,0:T(8,128)(2,1)S(1)} collective-permute-done((bf16[512,512]{1,0:T(8,128)(2,1)}, bf16[512,512]{1,0:T(8,128)(2,1)S(1)}, u32[]{:S(2)}, u32[]{:S(2)}) %collective-permute-start.13) | collective-permute-done | bytes 524320 | tf_op jit(solution)/shard_map/ppermute | solution.py:32
  82.3 0.8 fusion.13
  83.2 1.2 divide_convert_fusion
  84.4 0.1 collective-permute-start.16
  84.5 0.0 slice-start
  84.5 0.8 fusion.12
  85.3 0.0 slice-start.1
  85.3 1.2 divide_convert_fusion.1
  86.5 0.5 collective-permute-start.15
  87.0 0.1 pad_add_fusion.1.place
  87.1 1.5 %collective-permute-start.14 = (bf16[512,512]{1,0:T(8,128)(2,1)S(1)}, bf16[512,512]{1,0:T(8,128)(2,1)S(1)}, u32[]{:S(2)}, u32[]{:S(2)}) collective-permute-start(bf16[512,512]{1,0:T(8,128)(2,1)S(1)} %get-tuple-element.36.rest_1_), channel_id=1, source_target_pairs={{0,16},{8,24},{16,0},{24,8},{1,17},{9,25},{17,1},{25,9},{2,18},{10... | collective-permute-start | bytes 1572872 | tf_op jit(solution)/shard_map/ppermute | solution.py:32
  88.6 0.5 collective-permute-start.11
  89.2 2.6 %pad_maximum_fusion = (f32[1024,512]{1,0:T(8,128)}, f32[1024,512]{1,0:T(8,128)}) fusion(f32[512,512]{1,0:T(8,128)S(1)} %get-tuple-element.37, f32[512,512]{1,0:T(8,128)S(1)} %get-tuple-element.35, f32[512,512]{1,0:T(8,128)S(1)} %fusion.13, f32[512,512]{1,0:T(8,128)S(1)} %fusion.12), kind=kLoop, calls=%fused_computation.10 | loop fusion | flops 1048576 | bytes 8388608 | tf_op jit(solution)/shard_map/concatenate | solution.py:180
  91.8 1.1 copy-done.1
  92.9 7.6 %shard_map.93 = (bf16[2048,2048]{1,0:T(8,128)(2,1)}, bf16[2048,2048]{1,0:T(8,128)(2,1)}) custom-call(s32[2]{0:T(128)S(1)} %pad_add_fusion.1.place, bf16[2048,1024]{1,0:T(8,128)(2,1)S(1)} %copy-done.1, bf16[2048,2048]{1,0:T(8,128)(2,1)S(1)} %bitcast.47, bf16[512,512]{1,0:T(8,128)(2,1)S(1)} %get-tuple-element.34.rest_0_, ...), custom_call_target="tpu_custom_call" | custom-call | flops 4294967296 | bytes 18874368 | tf_op jit(solution)/shard_map/pallas_call | solution.py:112
  100.5 1.5 %collective-permute-done.14.rest_1_ = bf16[512,512]{1,0:T(8,128)(2,1)S(1)} collective-permute-done((bf16[512,512]{1,0:T(8,128)(2,1)S(1)}, bf16[512,512]{1,0:T(8,128)(2,1)S(1)}, u32[]{:S(2)}, u32[]{:S(2)}) %collective-permute-start.14) | collective-permute-done | bytes 524320 | tf_op jit(solution)/shard_map/ppermute | solution.py:32
  101.9 10.3 %collective-permute-done.11.rest_0_ = bf16[512,512]{1,0:T(8,128)(2,1)S(1)} collective-permute-done((bf16[512,512]{1,0:T(8,128)(2,1)S(1)}, bf16[512,512]{1,0:T(8,128)(2,1)S(1)}, u32[]{:S(2)}, u32[]{:S(2)}) %collective-permute-start.11) | collective-permute-done | bytes 524320 | tf_op jit(solution)/shard_map/ppermute | solution.py:32
  112.2 0.5 collective-permute-start.18
  112.7 0.1 pad_add_fusion.place
  112.8 1.3 %collective-permute-done.17.rest_2_ = bf16[512,512]{1,0:T(8,128)(2,1)S(1)} collective-permute-done((bf16[512,512]{1,0:T(8,128)(2,1)S(1)}, bf16[512,512]{1,0:T(8,128)(2,1)S(1)}, u32[]{:S(2)}, u32[]{:S(2)}) %collective-permute-start.17) | collective-permute-done | bytes 524320 | tf_op jit(solution)/shard_map/ppermute | solution.py:32
  114.1 0.7 collective-permute-done.18.rest_3_
  114.9 7.4 %shard_map.94 = (bf16[2048,2048]{1,0:T(8,128)(2,1)}, bf16[2048,2048]{1,0:T(8,128)(2,1)}) custom-call(s32[2]{0:T(128)S(1)} %pad_add_fusion.place, bf16[2048,1024]{1,0:T(8,128)(2,1)S(1)} %copy-done.1, bf16[2048,2048]{1,0:T(8,128)(2,1)S(1)} %bitcast.47, ...), custom_call_target="tpu_custom_call", output_to_operand_aliasing={{0}: (7, {}), {1}: (8, {})} | custom-call | flops 4294967296 | bytes 18874368 | tf_op jit(solution)/shard_map/pallas_call | solution.py:112
  (33 shorter events, 0.2 us)
Async XLA Ops:
  3.8 1.7 %collective-permute-start = (f32[64,1024]{1,0:T(8,128)S(1)}, f32[64,1024]{1,0:T(8,128)S(1)}, u32[]{:S(2)}, u32[]{:S(2)}) collective-permute-start(f32[64,1024]{1,0:T(8,128)S(1)} %constant_dynamic-slice_fusion.1), channel_id=1, source_target_pairs={{0,8},{8,0},{16,24},{24,16},{1,9},{9,1},{17,25},{25,17},{2,10},{10... | collective-permute-start | bytes 786440 | tf_op jit(solution)/shard_map/ppermute | solution.py:32
  10.9 2.0 %collective-permute-start.5 = (bf16[512,512]{1,0:T(8,128)(2,1)S(1)}, bf16[512,512]{1,0:T(8,128)(2,1)S(1)}, u32[]{:S(2)}, u32[]{:S(2)}) collective-permute-start(bf16[512,512]{1,0:T(8,128)(2,1)S(1)} %fusion.32), channel_id=1, source_target_pairs={{0,8},{8,0},{16,24},{24,16},{1,9},{9,1},{17,25},{25,17},{2,10},{10... | collective-permute-start | bytes 1572872 | tf_op jit(solution)/shard_map/ppermute | solution.py:32
  19.1 13.0 %collective-permute-start.6 = (bf16[512,512]{1,0:T(8,128)(2,1)S(1)}, bf16[512,512]{1,0:T(8,128)(2,1)S(1)}, u32[]{:S(2)}, u32[]{:S(2)}) collective-permute-start(bf16[512,512]{1,0:T(8,128)(2,1)S(1)} %fusion.33), channel_id=1, source_target_pairs={{0,8},{8,0},{16,24},{24,16},{1,9},{9,1},{17,25},{25,17},{2,10},{10... | collective-permute-start | bytes 1572872 | tf_op jit(solution)/shard_map/ppermute | solution.py:32
  19.6 6.7 %collective-permute-start.1 = (bf16[64,1024]{1,0:T(8,128)(2,1)S(1)}, bf16[64,1024]{1,0:T(8,128)(2,1)}, u32[]{:S(2)}, u32[]{:S(2)}) collective-permute-start(bf16[64,1024]{1,0:T(8,128)(2,1)S(1)} %get-tuple-element.32), channel_id=1, source_target_pairs={{0,16},{8,24},{16,0},{24,8},{1,17},{9,25},{17,1},{25,9},{2,18},{10... | collective-permute-start | bytes 393224 | tf_op jit(solution)/shard_map/ppermute | solution.py:32
  27.3 12.5 %collective-permute-start.4 = (bf16[64,1024]{1,0:T(8,128)(2,1)S(1)}, bf16[64,1024]{1,0:T(8,128)(2,1)S(1)}, u32[]{:S(2)}, u32[]{:S(2)}) collective-permute-start(bf16[64,1024]{1,0:T(8,128)(2,1)S(1)} %add_convert_fusion), channel_id=1, source_target_pairs={{0,6},{1,7},{2,0},{3,1},{4,2},{5,3},{6,4},{7,5},{8,14},{9,15},{10,... | collective-permute-start | bytes 393224 | tf_op jit(solution)/shard_map/ppermute | solution.py:58
  31.2 10.8 %collective-permute-start.3 = (bf16[64,1024]{1,0:T(8,128)(2,1)S(1)}, bf16[64,1024]{1,0:T(8,128)(2,1)S(1)}, u32[]{:S(2)}, u32[]{:S(2)}) collective-permute-start(bf16[64,1024]{1,0:T(8,128)(2,1)S(1)} %add_convert_fusion), channel_id=1, source_target_pairs={{0,4},{1,5},{2,6},{3,7},{4,0},{5,1},{6,2},{7,3},{8,12},{9,13},{10,... | collective-permute-start | bytes 393224 | tf_op jit(solution)/shard_map/ppermute | solution.py:58
  31.2 10.8 %collective-permute-start.2 = (bf16[64,1024]{1,0:T(8,128)(2,1)S(1)}, bf16[64,1024]{1,0:T(8,128)(2,1)S(1)}, u32[]{:S(2)}, u32[]{:S(2)}) collective-permute-start(bf16[64,1024]{1,0:T(8,128)(2,1)S(1)} %add_convert_fusion), channel_id=1, source_target_pairs={{0,2},{1,3},{2,4},{3,5},{4,6},{5,7},{6,0},{7,1},{8,10},{9,11},{10,... | collective-permute-start | bytes 393224 | tf_op jit(solution)/shard_map/ppermute | solution.py:58
  32.2 11.6 %slice-start.2 = ((s8[8388608]{0:T(1024)(128)(4,1)}), s8[4194304]{0:T(1024)(128)(4,1)S(1)}, s32[]{:S(2)}) async-start(s8[8388608]{0:T(1024)(128)(4,1)} %bitcast.56), calls=%async_computation.2 | async-start | bytes 8388608
  33.2 10.6 %slice-start.3 = ((s8[8388608]{0:T(1024)(128)(4,1)}), s8[4194304]{0:T(1024)(128)(4,1)S(1)}, s32[]{:S(2)}) async-start(s8[8388608]{0:T(1024)(128)(4,1)} %bitcast.56), calls=%async_computation.3 | async-start | bytes 8388608
  38.9 4.9 %copy-start = (bf16[2048,1024]{1,0:T(8,128)(2,1)S(1)}, bf16[2048,1024]{1,0:T(8,128)(2,1)}, u32[]{:S(2)}) copy-start(bf16[2048,1024]{1,0:T(8,128)(2,1)} %basis.3) | copy-start | bytes 12582916
  42.2 13.2 %collective-permute-start.7 = (bf16[4,64,1024]{2,1,0:T(8,128)(2,1)S(1)}, bf16[4,64,1024]{2,1,0:T(8,128)(2,1)S(1)}, u32[]{:S(2)}, u32[]{:S(2)}) collective-permute-start(bf16[4,64,1024]{2,1,0:T(8,128)(2,1)S(1)} %bitcast.50), channel_id=1, source_target_pairs={{0,1},{1,0},{2,3},{3,2},{4,5},{5,4},{6,7},{7,6},{8,9},{9,8},{10,11... | collective-permute-start | bytes 1572872 | tf_op jit(solution)/shard_map/ppermute | solution.py:32
  46.2 9.2 %copy-start.3 = (f32[1024,512]{0,1:T(8,128)}, f32[1024,512]{0,1:T(8,128)S(1)}, u32[]{:S(2)}) copy-start(f32[1024,512]{0,1:T(8,128)S(1)} %fusion) | copy-start | bytes 6291460
  56.5 3.0 %collective-permute-start.8 = (bf16[4,2,64,1024]{3,2,0,1:T(8,128)(2,1)}, bf16[4,2,64,1024]{3,2,0,1:T(8,128)(2,1)}, u32[]{:S(2)}, u32[]{:S(2)}) collective-permute-start(bf16[4,2,64,1024]{3,2,0,1:T(8,128)(2,1)} %maximum_select_fusion.1), channel_id=1, source_target_pairs={{0,8},{8,0},{16,24},{24,16},{1,9},{9,1},{17,25},{25,17},{2,10},{10... | collective-permute-start | bytes 3145736 | tf_op jit(solution)/shard_map/ppermute | solution.py:32
  56.5 27.9 %collective-permute-start.10 = (bf16[512,512]{1,0:T(8,128)(2,1)}, bf16[512,512]{1,0:T(8,128)(2,1)S(1)}, u32[]{:S(2)}, u32[]{:S(2)}) collective-permute-start(bf16[512,512]{1,0:T(8,128)(2,1)} %fusion.31), channel_id=1, source_target_pairs={{0,16},{8,24},{16,0},{24,8},{1,17},{9,25},{17,1},{25,9},{2,18},{10... | collective-permute-start | bytes 1572872 | tf_op jit(solution)/shard_map/ppermute | solution.py:32
  58.0 24.3 %collective-permute-start.13 = (bf16[512,512]{1,0:T(8,128)(2,1)}, bf16[512,512]{1,0:T(8,128)(2,1)S(1)}, u32[]{:S(2)}, u32[]{:S(2)}) collective-permute-start(bf16[512,512]{1,0:T(8,128)(2,1)} %fusion.30), channel_id=1, source_target_pairs={{0,16},{8,24},{16,0},{24,8},{1,17},{9,25},{17,1},{25,9},{2,18},{10... | collective-permute-start | bytes 1572872 | tf_op jit(solution)/shard_map/ppermute | solution.py:32
  58.6 25.9 %collective-permute-start.9 = (bf16[512,512]{1,0:T(8,128)(2,1)}, bf16[512,512]{1,0:T(8,128)(2,1)S(1)}, u32[]{:S(2)}, u32[]{:S(2)}) collective-permute-start(bf16[512,512]{1,0:T(8,128)(2,1)} %fusion.34), channel_id=1, source_target_pairs={{0,8},{8,0},{16,24},{24,16},{1,9},{9,1},{17,25},{25,17},{2,10},{10... | collective-permute-start | bytes 1572872 | tf_op jit(solution)/shard_map/ppermute | solution.py:32
  58.6 23.8 %collective-permute-start.12 = (bf16[512,512]{1,0:T(8,128)(2,1)}, bf16[512,512]{1,0:T(8,128)(2,1)S(1)}, u32[]{:S(2)}, u32[]{:S(2)}) collective-permute-start(bf16[512,512]{1,0:T(8,128)(2,1)} %fusion.35), channel_id=1, source_target_pairs={{0,8},{8,0},{16,24},{24,16},{1,9},{9,1},{17,25},{25,17},{2,10},{10... | collective-permute-start | bytes 1572872 | tf_op jit(solution)/shard_map/ppermute | solution.py:32
  61.1 21.3 %copy-start.2 = (f32[1024,512]{1,0:T(8,128)S(1)}, f32[1024,512]{1,0:T(8,128)}, u32[]{:S(2)}) copy-start(f32[1024,512]{1,0:T(8,128)} %param.11) | copy-start | bytes 6291460
  61.1 21.2 %copy-start.4 = (f32[1024,512]{0,1:T(8,128)S(1)}, f32[1024,512]{0,1:T(8,128)}, u32[]{:S(2)}) copy-start(f32[1024,512]{0,1:T(8,128)} %copy-done.3) | copy-start | bytes 6291460
  61.7 21.4 %copy-start.5 = (f32[1024,512]{1,0:T(8,128)S(1)}, f32[1024,512]{1,0:T(8,128)}, u32[]{:S(2)}) copy-start(f32[1024,512]{1,0:T(8,128)} %param.10) | copy-start | bytes 6291460
  84.4 7.4 %collective-permute-start.16 = (bf16[512,512]{1,0:T(8,128)(2,1)S(1)}, bf16[512,512]{1,0:T(8,128)(2,1)S(1)}, u32[]{:S(2)}, u32[]{:S(2)}) collective-permute-start(bf16[512,512]{1,0:T(8,128)(2,1)S(1)} %get-tuple-element.36.rest_1_), channel_id=1, source_target_pairs={{0,8},{8,0},{16,24},{24,16},{1,9},{9,1},{17,25},{25,17},{2,10},{10... | collective-permute-start | bytes 1572872 | tf_op jit(solution)/shard_map/ppermute | solution.py:32
  84.5 7.3 %slice-start = ((s8[8388608]{0:T(1024)(128)(4,1)}), s8[4194304]{0:T(1024)(128)(4,1)S(1)}, s32[]{:S(2)}) async-start(s8[8388608]{0:T(1024)(128)(4,1)} %bitcast.46), calls=%async_computation | async-start | bytes 8388608
  85.3 6.4 %slice-start.1 = ((s8[8388608]{0:T(1024)(128)(4,1)}), s8[4194304]{0:T(1024)(128)(4,1)S(1)}, s32[]{:S(2)}) async-start(s8[8388608]{0:T(1024)(128)(4,1)} %bitcast.46), calls=%async_computation.1 | async-start | bytes 8388608
  86.5 5.2 %collective-permute-start.15 = (bf16[512,512]{1,0:T(8,128)(2,1)S(1)}, bf16[512,512]{1,0:T(8,128)(2,1)S(1)}, u32[]{:S(2)}, u32[]{:S(2)}) collective-permute-start(bf16[512,512]{1,0:T(8,128)(2,1)S(1)} %get-tuple-element.34.rest_0_), channel_id=1, source_target_pairs={{0,8},{8,0},{16,24},{24,16},{1,9},{9,1},{17,25},{25,17},{2,10},{10... | collective-permute-start | bytes 1572872 | tf_op jit(solution)/shard_map/ppermute | solution.py:32
  87.1 14.8 %collective-permute-start.14 = (bf16[512,512]{1,0:T(8,128)(2,1)S(1)}, bf16[512,512]{1,0:T(8,128)(2,1)S(1)}, u32[]{:S(2)}, u32[]{:S(2)}) collective-permute-start(bf16[512,512]{1,0:T(8,128)(2,1)S(1)} %get-tuple-element.36.rest_1_), channel_id=1, source_target_pairs={{0,16},{8,24},{16,0},{24,8},{1,17},{9,25},{17,1},{25,9},{2,18},{10... | collective-permute-start | bytes 1572872 | tf_op jit(solution)/shard_map/ppermute | solution.py:32
  88.6 23.6 %collective-permute-start.11 = (bf16[512,512]{1,0:T(8,128)(2,1)S(1)}, bf16[512,512]{1,0:T(8,128)(2,1)S(1)}, u32[]{:S(2)}, u32[]{:S(2)}) collective-permute-start(bf16[512,512]{1,0:T(8,128)(2,1)S(1)} %get-tuple-element.34.rest_0_), channel_id=1, source_target_pairs={{0,16},{8,24},{16,0},{24,8},{1,17},{9,25},{17,1},{25,9},{2,18},{10... | collective-permute-start | bytes 1572872 | tf_op jit(solution)/shard_map/ppermute | solution.py:32
  89.2 3.7 %copy-start.1 = (bf16[2048,1024]{1,0:T(8,128)(2,1)S(1)}, bf16[2048,1024]{1,0:T(8,128)(2,1)}, u32[]{:S(2)}) copy-start(bf16[2048,1024]{1,0:T(8,128)(2,1)} %basis.3) | copy-start | bytes 12582916
  112.2 1.9 %collective-permute-start.17 = (bf16[512,512]{1,0:T(8,128)(2,1)S(1)}, bf16[512,512]{1,0:T(8,128)(2,1)S(1)}, u32[]{:S(2)}, u32[]{:S(2)}) collective-permute-start(bf16[512,512]{1,0:T(8,128)(2,1)S(1)} %collective-permute-done.11.rest_0_), channel_id=1, source_target_pairs={{0,8},{8,0},{16,24},{24,16},{1,9},{9,1},{17,25},{25,17},{2,10},{10... | collective-permute-start | bytes 1572872 | tf_op jit(solution)/shard_map/ppermute | solution.py:32
  112.2 2.7 %collective-permute-start.18 = (bf16[512,512]{1,0:T(8,128)(2,1)S(1)}, bf16[512,512]{1,0:T(8,128)(2,1)S(1)}, u32[]{:S(2)}, u32[]{:S(2)}) collective-permute-start(bf16[512,512]{1,0:T(8,128)(2,1)S(1)} %collective-permute-done.14.rest_1_), channel_id=1, source_target_pairs={{0,8},{8,0},{16,24},{24,16},{1,9},{9,1},{17,25},{25,17},{2,10},{10... | collective-permute-start | bytes 1572872 | tf_op jit(solution)/shard_map/ppermute | solution.py:32
where the time goes:
time: 122 us
  waiting for transfers between devices  52 us (43%)
  matrix products  25.7 us (21%)
  starting transfers between devices  16.2 us (13%)
  Pallas kernels  15 us (12%)
  other arithmetic  7.68 us (6%)
  local copies, waits for them, and re-layouts  4.68 us (4%)
    ppermute x16, waiting for transfers between devices, swap(): return lax.ppermute(values, axis, [(k, k ^ bit) for k in range(size)])  49.8 us
    dot_general x9, matrix products, product(): jnp.einsum('mr,mn->rn', left, right, preferred_element_type=jnp.float32)  25.7 us
    pallas_call x2, Pallas kernels, back_half(): pl.pallas_call(functools.partial(back_kernel, width, len(mine)), out_shap...  15 us
    ppermute x16, starting transfers between devices, swap(): return lax.ppermute(values, axis, [(k, k ^ bit) for k in range(size)])  11.3 us
    ppermute x3, starting transfers between devices, along_layers(): lax.ppermute(piece, 'col', [(k, (k + 2 * hop) % columns) for k in range(c...  4.92 us
    convert_element_type x5, other arithmetic, low(): return values.astype(jnp.bfloat16)  3.53 us
    concatenate x1, other arithmetic, paired(): jnp.concatenate([step[k] for step in steps])  2.58 us
  transfers between devices with their start and end apart: 19, of which 11 were waited for; matrix products, arithmetic and copies ran while one was open for 17% of the time, Pallas kernels for 6%

commit v1 on v0

--- a/solution.py
+++ b/solution.py
@@ -162,17 +162,21 @@
         from_core.append(swap(mate, "row", rows, 1))
         if k == 0:
             along = layers_in_order(piece, after(received, mate))
-            beyond = swap(along, "col", columns, 1)
+            along = [along[:, :, each] for each in parts]
+            beyond = []
+            for values in along:
+                beyond.append(swap(values, "col", columns, 1))
             source = after(gradient, along)
-    both = in_order(along, after(beyond, mate), lax.axis_index("col") & 1, 1)
-    flipped = in_order(both, swap(both, "row", rows, 1), core_at, 2)
-    flipped = flipped.reshape(old_basis.shape[1], new_basis.shape[1])
-    squares = low(jnp.square(wide(flipped)))
     first_moment, second_moment = low(first_moment), low(second_moment)
     steps, across = [], []
-    for k, part in enumerate(parts):
+    earlier = mate
+    for k in range(CHUNKS):
+        both = in_order(along[k], after(beyond[k], earlier), lax.axis_index("col") & 1, 1)
+        flipped = in_order(both, swap(both, "row", rows, 1), core_at, 2).reshape(-1, chunk)
+        squares = low(jnp.square(wide(flipped)))
         projected = near[k] + wide(from_core[k]) + wide(from_chip[k])
-        steps.append(stepped(flipped[:, part], squares[:, part], first_moment, second_moment, projected))
+        steps.append(stepped(flipped, squares, first_moment, second_moment, projected))
+        earlier = steps[k][2]
         across.append(swap(steps[k][2], "row", rows, 2))
     direction = [step[2] for step in steps]
     beside = [swap(values, "row", rows, 1) for values in direction]

time: 122 us -> 123 us (level)
  waiting for transfers between devices: 52 us -> 47.6 us
  matrix products: 25.7 us -> 28.3 us
  starting transfers between devices: 16.2 us -> 18.6 us
    ppermute x16 -> x18, waiting for transfers between devices: 49.8 us -> 45.5 us  [swap(): return lax.ppermute(values, axis, [(k, k ^ bit) for k in range(size)])]
    dot_general x9, matrix products: 25.7 us -> 28.3 us  [product(): jnp.einsum('mr,mn->rn', left, right, preferred_element_type=jnp.float32)]
    ppermute x16 -> x18, starting transfers between devices: 11.3 us -> 13.6 us  [swap(): return lax.ppermute(values, axis, [(k, k ^ bit) for k in range(size)])]
    convert_element_type x5 -> x4, other arithmetic: 3.53 us -> 2.86 us  [low(): return values.astype(jnp.bfloat16)]
  transfers between devices with their start and end apart: 19 -> 21, of which waited for: 11 -> 11; matrix products, arithmetic and copies ran while one was open for 17% -> 19% of each run, Pallas kernels for 6% -> 6%
where the time goes in v1:
time: 123 us; the launch traced here: 122 us
  waiting for transfers between devices  47.6 us (39%)
  matrix products  28.3 us (23%)
  starting transfers between devices  18.6 us (15%)
  Pallas kernels  15 us (12%)
  other arithmetic  7 us (6%)
  local copies, waits for them, and re-layouts  5.05 us (4%)
    ppermute x18, waiting for transfers between devices, swap(): return lax.ppermute(values, axis, [(k, k ^ bit) for k in range(size)])  45.5 us
    dot_general x9, matrix products, product(): jnp.einsum('mr,mn->rn', left, right, preferred_element_type=jnp.float32)  28.3 us
    pallas_call x2, Pallas kernels, back_half(): pl.pallas_call(functools.partial(back_kernel, width, len(mine)), out_shap...  15 us
    ppermute x18, starting transfers between devices, swap(): return lax.ppermute(values, axis, [(k, k ^ bit) for k in range(size)])  13.6 us
    ppermute x3, starting transfers between devices, along_layers(): lax.ppermute(piece, 'col', [(k, (k + 2 * hop) % columns) for k in range(c...  4.92 us
    convert_element_type x4, other arithmetic, low(): return values.astype(jnp.bfloat16)  2.86 us
    concatenate x1, other arithmetic, paired(): jnp.concatenate([step[k] for step in steps])  2.64 us
  transfers between devices with their start and end apart: 21, of which 11 were waited for; matrix products, arithmetic and copies ran while one was open for 19% of the time, Pallas kernels for 6%

profile of v1, /device:TPU:0, one launch (start us, length us, event | category | flops | bytes accessed | tf_op | source)
XLA Modules:
  0.0 122.5 jit_solution(10161932462744597622)
XLA Ops:
  0.6 3.1 %fusion.26 = f32[128,1024]{1,0:T(8,128)S(1)} fusion(bf16[2048,1024]{1,0:T(8,128)(2,1)} %basis.3, bf16[2048,1024]{1,0:T(8,128)(2,1)} %param.8, s32[]{:T(128)S(6)} %select_n.91), kind=kOutput, calls=%fused_computation.55 | convolution fusion | flops 536870912 | bytes 5242884 | tf_op jit(solution)/shard_map/mr,mn->rn/dot_general | solution.py:28
  3.8 0.6 collective-permute-start
  4.4 1.2 collective-permute-done
  5.6 5.2 %fusion.6 = f32[1024,512]{0,1:T(8,128)S(1)} fusion(bf16[2048,2048]{1,0:T(8,128)(2,1)} %param.7, s32[]{:T(128)S(6)} %select_n.94, bf16[2048,1024]{1,0:T(8,128)(2,1)} %basis.3), kind=kOutput, calls=%fused_computation.6 | convolution fusion | flops 2147483648 | bytes 8388612 | tf_op jit(solution)/shard_map/mr,mn->rn/dot_general | solution.py:28
  10.8 0.1 fusion.18
  10.9 0.4 collective-permute-start.5
  11.3 1.5 %collective-permute-done.5 = bf16[512,512]{1,0:T(8,128)(2,1)S(1)} collective-permute-done((bf16[512,512]{1,0:T(8,128)(2,1)S(1)}, bf16[512,512]{1,0:T(8,128)(2,1)S(1)}, u32[]{:S(2)}, u32[]{:S(2)}) %collective-permute-start.5) | collective-permute-done | bytes 524320 | tf_op jit(solution)/shard_map/ppermute | solution.py:32
  12.9 1.0 fusion.17
  13.8 5.2 %fusion.4 = f32[1024,512]{0,1:T(8,128)S(1)} fusion(bf16[2048,2048]{1,0:T(8,128)(2,1)} %param.7, s32[]{:T(128)S(6)} %select_n.94, bf16[2048,1024]{1,0:T(8,128)(2,1)} %basis.3), kind=kOutput, calls=%fused_computation.4 | convolution fusion | flops 2147483648 | bytes 8388612 | tf_op jit(solution)/shard_map/mr,mn->rn/dot_general | solution.py:28
  19.1 0.1 fusion.19
  19.1 0.4 collective-permute-start.6
  19.6 2.6 %collective-permute-start.1 = (bf16[64,1024]{1,0:T(8,128)(2,1)S(1)}, bf16[64,1024]{1,0:T(8,128)(2,1)}, u32[]{:S(2)}, u32[]{:S(2)}) collective-permute-start(bf16[64,1024]{1,0:T(8,128)(2,1)S(1)} %get-tuple-element.34), channel_id=1, source_target_pairs={{0,16},{8,24},{16,0},{24,8},{1,17},{9,25},{17,1},{25,9},{2,18},{10... | collective-permute-start | bytes 393224 | tf_op jit(solution)/shard_map/ppermute | solution.py:32
  22.2 4.1 %collective-permute-done.1 = bf16[64,1024]{1,0:T(8,128)(2,1)} collective-permute-done((bf16[64,1024]{1,0:T(8,128)(2,1)S(1)}, bf16[64,1024]{1,0:T(8,128)(2,1)}, u32[]{:S(2)}, u32[]{:S(2)}) %collective-permute-start.1) | collective-permute-done | bytes 131104 | tf_op jit(solution)/shard_map/ppermute | solution.py:32
  26.3 0.9 add_convert_fusion
  27.3 3.9 %collective-permute-start.4 = (bf16[64,1024]{1,0:T(8,128)(2,1)S(1)}, bf16[64,1024]{1,0:T(8,128)(2,1)S(1)}, u32[]{:S(2)}, u32[]{:S(2)}) collective-permute-start(bf16[64,1024]{1,0:T(8,128)(2,1)S(1)} %add_convert_fusion), channel_id=1, source_target_pairs={{0,6},{1,7},{2,0},{3,1},{4,2},{5,3},{6,4},{7,5},{8,14},{9,15},{10,... | collective-permute-start | bytes 393224 | tf_op jit(solution)/shard_map/ppermute | solution.py:58
  31.2 1.0 collective-permute-start.2
  32.2 0.9 fusion.16
  33.1 5.7 %fusion.2 = f32[1024,512]{0,1:T(8,128)S(1)} fusion(bf16[2048,2048]{1,0:T(8,128)(2,1)} %param.7, s32[]{:T(128)S(6)} %select_n.97, bf16[2048,1024]{1,0:T(8,128)(2,1)} %basis.3), kind=kOutput, calls=%fused_computation.2 | convolution fusion | flops 2147483648 | bytes 8388612 | tf_op jit(solution)/shard_map/mr,mn->rn/dot_general | solution.py:28
  38.9 0.0 copy-start.3
  38.9 1.0 fusion.20
  39.8 2.1 %collective-permute-done.3 = bf16[64,1024]{1,0:T(8,128)(2,1)S(1)} collective-permute-done((bf16[64,1024]{1,0:T(8,128)(2,1)S(1)}, bf16[64,1024]{1,0:T(8,128)(2,1)S(1)}, u32[]{:S(2)}, u32[]{:S(2)}) %collective-permute-start.3) | collective-permute-done | bytes 131104 | tf_op jit(solution)/shard_map/ppermute | solution.py:58
  42.1 0.0 copy-start
  42.2 0.2 slice_bitcast_fusion.1
  42.4 1.6 %collective-permute-start.7 = (bf16[4,64,512]{2,1,0:T(8,128)(2,1)S(1)}, bf16[4,64,512]{2,1,0:T(8,128)(2,1)S(1)}, u32[]{:S(2)}, u32[]{:S(2)}) collective-permute-start(bf16[4,64,512]{2,1,0:T(8,128)(2,1)S(1)} %get-tuple-element.41), channel_id=1, source_target_pairs={{0,1},{1,0},{2,3},{3,2},{4,5},{5,4},{6,7},{7,6},{8,9},{9,8},{10,11... | collective-permute-start | bytes 786440 | tf_op jit(solution)/shard_map/ppermute | solution.py:32
  44.0 0.3 copy-done
  44.3 2.4 %fusion = f32[1024,512]{0,1:T(8,128)S(1)} fusion(bf16[2048,2048]{1,0:T(8,128)(2,1)S(1)} %bitcast.71, s32[]{:T(128)S(6)} %select_n.97, bf16[2048,1024]{1,0:T(8,128)(2,1)S(1)} %copy-done), kind=kOutput, calls=%fused_computation | convolution fusion | flops 2147483648 | bytes 8388612 | tf_op jit(solution)/shard_map/mr,mn->rn/dot_general | solution.py:28
  46.6 0.9 fusion.21
  47.5 2.4 %collective-permute-done.7 = bf16[4,64,512]{2,1,0:T(8,128)(2,1)S(1)} collective-permute-done((bf16[4,64,512]{2,1,0:T(8,128)(2,1)S(1)}, bf16[4,64,512]{2,1,0:T(8,128)(2,1)S(1)}, u32[]{:S(2)}, u32[]{:S(2)}) %collective-permute-start.7) | collective-permute-done | bytes 262176 | tf_op jit(solution)/shard_map/ppermute | solution.py:32
  50.0 0.9 maximum_select_fusion.2
  50.8 1.5 %collective-permute-start.10 = (bf16[512,512]{1,0:T(8,128)(2,1)}, bf16[512,512]{1,0:T(8,128)(2,1)}, u32[]{:S(2)}, u32[]{:S(2)}) collective-permute-start(bf16[512,512]{1,0:T(8,128)(2,1)} %fusion.17), channel_id=1, source_target_pairs={{0,16},{8,24},{16,0},{24,8},{1,17},{9,25},{17,1},{25,9},{2,18},{10... | collective-permute-start | bytes 1572872 | tf_op jit(solution)/shard_map/ppermute | solution.py:32
  52.3 0.2 collective-permute-start.9
  52.6 1.5 %collective-permute-start.12 = (bf16[4,64,512]{2,1,0:T(8,128)(2,1)S(1)}, bf16[4,64,512]{2,1,0:T(8,128)(2,1)S(1)}, u32[]{:S(2)}, u32[]{:S(2)}) collective-permute-start(bf16[4,64,512]{2,1,0:T(8,128)(2,1)S(1)} %get-tuple-element.40), channel_id=1, source_target_pairs={{0,1},{1,0},{2,3},{3,2},{4,5},{5,4},{6,7},{7,6},{8,9},{9,8},{10,11... | collective-permute-start | bytes 786440 | tf_op jit(solution)/shard_map/ppermute | solution.py:32
  54.2 1.2 %copy.29 = bf16[4,2,64,512]{3,2,1,0:T(8,128)(2,1)S(1)} copy(bf16[4,2,64,512]{3,2,0,1:T(8,128)(2,1)} %collective-permute-done.8) | data formatting | bytes 1048576 | tf_op jit(solution)/shard_map/ppermute | solution.py:32
  55.4 0.1 maximum_select_fusion
  55.5 10.0 %collective-permute-done.10 = bf16[512,512]{1,0:T(8,128)(2,1)} collective-permute-done((bf16[512,512]{1,0:T(8,128)(2,1)}, bf16[512,512]{1,0:T(8,128)(2,1)}, u32[]{:S(2)}, u32[]{:S(2)}) %collective-permute-start.10) | collective-permute-done | bytes 524320 | tf_op jit(solution)/shard_map/ppermute | solution.py:32
  65.5 0.0 copy-start.7
  65.5 2.2 %fusion.12 = f32[512,512]{1,0:T(8,128)S(1)} fusion(bf16[1024,512]{1,0:T(8,128)(2,1)S(1)} %bitcast.59, f32[1024,512]{1,0:T(8,128)S(1)} %copy-done.2, bf16[512,512]{1,0:T(8,128)(2,1)} %collective-permute-done.10, bf16[512,512]{1,0:T(8,128)(2,1)} %collective-permute-done.9, f32[1024,512]{0,1:T(8,128)S(1)} %copy-done.4, s32[]{:T(128)S(6)} %select_n.95), kind=kOutput, calls=%fused_computation.22 | convolution fusion | flops 541065216 | bytes 6291460 | tf_op jit(solution)/shard_map/mr,mn->rn/dot_general | solution.py:28
  67.7 2.5 %divide_convert_fusion.1 = (bf16[512,512]{1,0:T(8,128)(2,1)S(1)}, f32[512,512]{1,0:T(8,128)S(1)}) fusion(f32[512,512]{1,0:T(8,128)S(1)} %fusion.12, bf16[512,512]{1,0:T(8,128)(2,1)} %collective-permute-done.10, bf16[512,512]{1,0:T(8,128)(2,1)} %collective-permute-done.9, f32[1024,512]{0,1:T(8,128)S(1)} %copy-done.4, s32[]{:T(128)S(6)} %select_n.95, ...), kind=kOutput, calls=%fused_computation.36 | convolution fusion | flops 540016640 | bytes 7864324 | tf_op jit(solution)/shard_map/mr,mn->rn/dot_general | solution.py:28
  70.2 0.1 maximum_select_fusion.4
  70.3 0.1 collective-permute-start.13
  70.4 1.6 %collective-permute-start.15 = (bf16[512,512]{1,0:T(8,128)(2,1)S(1)}, bf16[512,512]{1,0:T(8,128)(2,1)S(1)}, u32[]{:S(2)}, u32[]{:S(2)}) collective-permute-start(bf16[512,512]{1,0:T(8,128)(2,1)S(1)} %copy-done.5), channel_id=1, source_target_pairs={{0,16},{8,24},{16,0},{24,8},{1,17},{9,25},{17,1},{25,9},{2,18},{10... | collective-permute-start | bytes 1572872 | tf_op jit(solution)/shard_map/ppermute | solution.py:32
  72.0 0.1 collective-permute-start.14
  72.1 0.4 collective-permute-start.17
  72.5 0.1 maximum_select_fusion.5
  72.6 0.2 maximum_select_fusion.1
  72.8 0.1 copy.25
  72.9 11.9 %collective-permute-done.15 = bf16[512,512]{1,0:T(8,128)(2,1)S(1)} collective-permute-done((bf16[512,512]{1,0:T(8,128)(2,1)S(1)}, bf16[512,512]{1,0:T(8,128)(2,1)S(1)}, u32[]{:S(2)}, u32[]{:S(2)}) %collective-permute-start.15) | collective-permute-done | bytes 524320 | tf_op jit(solution)/shard_map/ppermute | solution.py:32
  84.7 0.8 fusion.13
  85.6 0.0 slice-start.1
  85.6 1.1 divide_convert_fusion
  86.7 0.1 collective-permute-start.18
  86.8 0.1 pad_add_fusion.1.place
  86.9 1.5 %collective-permute-start.11 = (bf16[512,512]{1,0:T(8,128)(2,1)S(1)}, bf16[512,512]{1,0:T(8,128)(2,1)S(1)}, u32[]{:S(2)}, u32[]{:S(2)}) collective-permute-start(bf16[512,512]{1,0:T(8,128)(2,1)S(1)} %get-tuple-element.42.rest_0_), channel_id=1, source_target_pairs={{0,16},{8,24},{16,0},{24,8},{1,17},{9,25},{17,1},{25,9},{2,18},{10... | collective-permute-start | bytes 1572872 | tf_op jit(solution)/shard_map/ppermute | solution.py:32
  88.4 0.5 collective-permute-start.16
  88.9 2.6 %pad_maximum_fusion = (f32[1024,512]{1,0:T(8,128)}, f32[1024,512]{1,0:T(8,128)}) fusion(f32[512,512]{1,0:T(8,128)S(1)} %get-tuple-element.45, f32[512,512]{1,0:T(8,128)S(1)} %get-tuple-element.43, f32[512,512]{1,0:T(8,128)S(1)} %fusion.13, f32[512,512]{1,0:T(8,128)S(1)} %fusion.12), kind=kLoop, calls=%fused_computation.8 | loop fusion | flops 1048576 | bytes 8388608 | tf_op jit(solution)/shard_map/concatenate | solution.py:184
  91.6 1.0 copy-done.1
  92.6 7.6 %shard_map.93 = (bf16[2048,2048]{1,0:T(8,128)(2,1)}, bf16[2048,2048]{1,0:T(8,128)(2,1)}) custom-call(s32[2]{0:T(128)S(1)} %pad_add_fusion.1.place, bf16[2048,1024]{1,0:T(8,128)(2,1)S(1)} %copy-done.1, bf16[2048,2048]{1,0:T(8,128)(2,1)S(1)} %bitcast.58, bf16[512,512]{1,0:T(8,128)(2,1)S(1)} %get-tuple-element.42.rest_0_, ...), custom_call_target="tpu_custom_call" | custom-call | flops 4294967296 | bytes 18874368 | tf_op jit(solution)/shard_map/pallas_call | solution.py:112
  100.2 1.5 %collective-permute-done.11.rest_0_ = bf16[512,512]{1,0:T(8,128)(2,1)S(1)} collective-permute-done((bf16[512,512]{1,0:T(8,128)(2,1)S(1)}, bf16[512,512]{1,0:T(8,128)(2,1)S(1)}, u32[]{:S(2)}, u32[]{:S(2)}) %collective-permute-start.11) | collective-permute-done | bytes 524320 | tf_op jit(solution)/shard_map/ppermute | solution.py:32
  101.7 10.8 %collective-permute-done.16.rest_1_ = bf16[512,512]{1,0:T(8,128)(2,1)S(1)} collective-permute-done((bf16[512,512]{1,0:T(8,128)(2,1)S(1)}, bf16[512,512]{1,0:T(8,128)(2,1)S(1)}, u32[]{:S(2)}, u32[]{:S(2)}) %collective-permute-start.16) | collective-permute-done | bytes 524320 | tf_op jit(solution)/shard_map/ppermute | solution.py:32
  112.4 0.5 collective-permute-start.20
  113.0 0.1 pad_add_fusion.place
  113.0 1.3 %collective-permute-done.19.rest_2_ = bf16[512,512]{1,0:T(8,128)(2,1)S(1)} collective-permute-done((bf16[512,512]{1,0:T(8,128)(2,1)S(1)}, bf16[512,512]{1,0:T(8,128)(2,1)S(1)}, u32[]{:S(2)}, u32[]{:S(2)}) %collective-permute-start.19) | collective-permute-done | bytes 524320 | tf_op jit(solution)/shard_map/ppermute | solution.py:32
  114.4 0.7 collective-permute-done.20.rest_3_
  115.1 7.4 %shard_map.94 = (bf16[2048,2048]{1,0:T(8,128)(2,1)}, bf16[2048,2048]{1,0:T(8,128)(2,1)}) custom-call(s32[2]{0:T(128)S(1)} %pad_add_fusion.place, bf16[2048,1024]{1,0:T(8,128)(2,1)S(1)} %copy-done.1, bf16[2048,2048]{1,0:T(8,128)(2,1)S(1)} %bitcast.58, ...), custom_call_target="tpu_custom_call", output_to_operand_aliasing={{0}: (7, {}), {1}: (8, {})} | custom-call | flops 4294967296 | bytes 18874368 | tf_op jit(solution)/shard_map/pallas_call | solution.py:112
  (45 shorter events, 0.3 us)
Async XLA Ops:
  3.8 1.7 %collective-permute-start = (f32[64,1024]{1,0:T(8,128)S(1)}, f32[64,1024]{1,0:T(8,128)S(1)}, u32[]{:S(2)}, u32[]{:S(2)}) collective-permute-start(f32[64,1024]{1,0:T(8,128)S(1)} %constant_dynamic-slice_fusion.1), channel_id=1, source_target_pairs={{0,8},{8,0},{16,24},{24,16},{1,9},{9,1},{17,25},{25,17},{2,10},{10... | collective-permute-start | bytes 786440 | tf_op jit(solution)/shard_map/ppermute | solution.py:32
  10.9 2.0 %collective-permute-start.5 = (bf16[512,512]{1,0:T(8,128)(2,1)S(1)}, bf16[512,512]{1,0:T(8,128)(2,1)S(1)}, u32[]{:S(2)}, u32[]{:S(2)}) collective-permute-start(bf16[512,512]{1,0:T(8,128)(2,1)S(1)} %fusion.18), channel_id=1, source_target_pairs={{0,8},{8,0},{16,24},{24,16},{1,9},{9,1},{17,25},{25,17},{2,10},{10... | collective-permute-start | bytes 1572872 | tf_op jit(solution)/shard_map/ppermute | solution.py:32
  19.1 13.0 %collective-permute-start.6 = (bf16[512,512]{1,0:T(8,128)(2,1)S(1)}, bf16[512,512]{1,0:T(8,128)(2,1)S(1)}, u32[]{:S(2)}, u32[]{:S(2)}) collective-permute-start(bf16[512,512]{1,0:T(8,128)(2,1)S(1)} %fusion.19), channel_id=1, source_target_pairs={{0,8},{8,0},{16,24},{24,16},{1,9},{9,1},{17,25},{25,17},{2,10},{10... | collective-permute-start | bytes 1572872 | tf_op jit(solution)/shard_map/ppermute | solution.py:32
  19.6 6.7 %collective-permute-start.1 = (bf16[64,1024]{1,0:T(8,128)(2,1)S(1)}, bf16[64,1024]{1,0:T(8,128)(2,1)}, u32[]{:S(2)}, u32[]{:S(2)}) collective-permute-start(bf16[64,1024]{1,0:T(8,128)(2,1)S(1)} %get-tuple-element.34), channel_id=1, source_target_pairs={{0,16},{8,24},{16,0},{24,8},{1,17},{9,25},{17,1},{25,9},{2,18},{10... | collective-permute-start | bytes 393224 | tf_op jit(solution)/shard_map/ppermute | solution.py:32
  27.3 12.6 %collective-permute-start.4 = (bf16[64,1024]{1,0:T(8,128)(2,1)S(1)}, bf16[64,1024]{1,0:T(8,128)(2,1)S(1)}, u32[]{:S(2)}, u32[]{:S(2)}) collective-permute-start(bf16[64,1024]{1,0:T(8,128)(2,1)S(1)} %add_convert_fusion), channel_id=1, source_target_pairs={{0,6},{1,7},{2,0},{3,1},{4,2},{5,3},{6,4},{7,5},{8,14},{9,15},{10,... | collective-permute-start | bytes 393224 | tf_op jit(solution)/shard_map/ppermute | solution.py:58
  31.2 10.8 %collective-permute-start.3 = (bf16[64,1024]{1,0:T(8,128)(2,1)S(1)}, bf16[64,1024]{1,0:T(8,128)(2,1)S(1)}, u32[]{:S(2)}, u32[]{:S(2)}) collective-permute-start(bf16[64,1024]{1,0:T(8,128)(2,1)S(1)} %add_convert_fusion), channel_id=1, source_target_pairs={{0,4},{1,5},{2,6},{3,7},{4,0},{5,1},{6,2},{7,3},{8,12},{9,13},{10,... | collective-permute-start | bytes 393224 | tf_op jit(solution)/shard_map/ppermute | solution.py:58
  31.2 10.8 %collective-permute-start.2 = (bf16[64,1024]{1,0:T(8,128)(2,1)S(1)}, bf16[64,1024]{1,0:T(8,128)(2,1)S(1)}, u32[]{:S(2)}, u32[]{:S(2)}) collective-permute-start(bf16[64,1024]{1,0:T(8,128)(2,1)S(1)} %add_convert_fusion), channel_id=1, source_target_pairs={{0,2},{1,3},{2,4},{3,5},{4,6},{5,7},{6,0},{7,1},{8,10},{9,11},{10,... | collective-permute-start | bytes 393224 | tf_op jit(solution)/shard_map/ppermute | solution.py:58
  32.2 11.8 %slice-start.2 = ((s8[8388608]{0:T(1024)(128)(4,1)}), s8[4194304]{0:T(1024)(128)(4,1)S(1)}, s32[]{:S(2)}) async-start(s8[8388608]{0:T(1024)(128)(4,1)} %bitcast.70), calls=%async_computation.2 | async-start | bytes 8388608
  33.1 10.8 %slice-start.3 = ((s8[8388608]{0:T(1024)(128)(4,1)}), s8[4194304]{0:T(1024)(128)(4,1)S(1)}, s32[]{:S(2)}) async-start(s8[8388608]{0:T(1024)(128)(4,1)} %bitcast.70), calls=%async_computation.3 | async-start | bytes 8388608
  38.9 3.2 %copy-start.3 = (f32[1024,512]{0,1:T(8,128)}, f32[1024,512]{0,1:T(8,128)S(1)}, u32[]{:S(2)}) copy-start(f32[1024,512]{0,1:T(8,128)S(1)} %fusion.2) | copy-start | bytes 6291460
  42.1 2.2 %copy-start = (bf16[2048,1024]{1,0:T(8,128)(2,1)S(1)}, bf16[2048,1024]{1,0:T(8,128)(2,1)}, u32[]{:S(2)}) copy-start(bf16[2048,1024]{1,0:T(8,128)(2,1)} %basis.3) | copy-start | bytes 12582916
  42.4 7.6 %collective-permute-start.7 = (bf16[4,64,512]{2,1,0:T(8,128)(2,1)S(1)}, bf16[4,64,512]{2,1,0:T(8,128)(2,1)S(1)}, u32[]{:S(2)}, u32[]{:S(2)}) collective-permute-start(bf16[4,64,512]{2,1,0:T(8,128)(2,1)S(1)} %get-tuple-element.41), channel_id=1, source_target_pairs={{0,1},{1,0},{2,3},{3,2},{4,5},{5,4},{6,7},{7,6},{8,9},{9,8},{10,11... | collective-permute-start | bytes 786440 | tf_op jit(solution)/shard_map/ppermute | solution.py:32
  50.8 3.3 %collective-permute-start.8 = (bf16[4,2,64,512]{3,2,0,1:T(8,128)(2,1)}, bf16[4,2,64,512]{3,2,0,1:T(8,128)(2,1)}, u32[]{:S(2)}, u32[]{:S(2)}) collective-permute-start(bf16[4,2,64,512]{3,2,0,1:T(8,128)(2,1)} %maximum_select_fusion.2), channel_id=1, source_target_pairs={{0,8},{8,0},{16,24},{24,16},{1,9},{9,1},{17,25},{25,17},{2,10},{10... | collective-permute-start | bytes 1572872 | tf_op jit(solution)/shard_map/ppermute | solution.py:32
  50.8 14.7 %collective-permute-start.10 = (bf16[512,512]{1,0:T(8,128)(2,1)}, bf16[512,512]{1,0:T(8,128)(2,1)}, u32[]{:S(2)}, u32[]{:S(2)}) collective-permute-start(bf16[512,512]{1,0:T(8,128)(2,1)} %fusion.17), channel_id=1, source_target_pairs={{0,16},{8,24},{16,0},{24,8},{1,17},{9,25},{17,1},{25,9},{2,18},{10... | collective-permute-start | bytes 1572872 | tf_op jit(solution)/shard_map/ppermute | solution.py:32
  52.3 13.2 %collective-permute-start.9 = (bf16[512,512]{1,0:T(8,128)(2,1)}, bf16[512,512]{1,0:T(8,128)(2,1)}, u32[]{:S(2)}, u32[]{:S(2)}) collective-permute-start(bf16[512,512]{1,0:T(8,128)(2,1)} %fusion.20), channel_id=1, source_target_pairs={{0,8},{8,0},{16,24},{24,16},{1,9},{9,1},{17,25},{25,17},{2,10},{10... | collective-permute-start | bytes 1572872 | tf_op jit(solution)/shard_map/ppermute | solution.py:32
  52.6 17.7 %collective-permute-start.12 = (bf16[4,64,512]{2,1,0:T(8,128)(2,1)S(1)}, bf16[4,64,512]{2,1,0:T(8,128)(2,1)S(1)}, u32[]{:S(2)}, u32[]{:S(2)}) collective-permute-start(bf16[4,64,512]{2,1,0:T(8,128)(2,1)S(1)} %get-tuple-element.40), channel_id=1, source_target_pairs={{0,1},{1,0},{2,3},{3,2},{4,5},{5,4},{6,7},{7,6},{8,9},{9,8},{10,11... | collective-permute-start | bytes 786440 | tf_op jit(solution)/shard_map/ppermute | solution.py:32
  54.1 11.4 %copy-start.2 = (f32[1024,512]{1,0:T(8,128)S(1)}, f32[1024,512]{1,0:T(8,128)}, u32[]{:S(2)}) copy-start(f32[1024,512]{1,0:T(8,128)} %param.11) | copy-start | bytes 6291460
  54.1 11.4 %copy-start.4 = (f32[1024,512]{0,1:T(8,128)S(1)}, f32[1024,512]{0,1:T(8,128)}, u32[]{:S(2)}) copy-start(f32[1024,512]{0,1:T(8,128)} %copy-done.3) | copy-start | bytes 6291460
  65.5 2.2 %copy-start.7 = (f32[1024,512]{1,0:T(8,128)S(1)}, f32[1024,512]{1,0:T(8,128)}, u32[]{:S(2)}) copy-start(f32[1024,512]{1,0:T(8,128)} %param.10) | copy-start | bytes 6291460
  67.7 2.7 %copy-start.5 = (bf16[512,512]{1,0:T(8,128)(2,1)S(1)}, bf16[512,512]{1,0:T(8,128)(2,1)}, u32[]{:S(2)}) copy-start(bf16[512,512]{1,0:T(8,128)(2,1)} %fusion.16) | copy-start | bytes 1572868
  67.7 4.2 %copy-start.6 = (bf16[512,512]{1,0:T(8,128)(2,1)S(1)}, bf16[512,512]{1,0:T(8,128)(2,1)}, u32[]{:S(2)}) copy-start(bf16[512,512]{1,0:T(8,128)(2,1)} %fusion.21) | copy-start | bytes 1572868
  70.3 2.2 %collective-permute-start.13 = (bf16[4,2,64,512]{3,2,0,1:T(8,128)(2,1)S(1)}, bf16[4,2,64,512]{3,2,0,1:T(8,128)(2,1)S(1)}, u32[]{:S(2)}, u32[]{:S(2)}) collective-permute-start(bf16[4,2,64,512]{3,2,0,1:T(8,128)(2,1)S(1)} %maximum_select_fusion.4), channel_id=1, source_target_pairs={{0,8},{8,0},{16,24},{24,16},{1,9},{9,1},{17,25},{25,17},{2,10},{10... | collective-permute-start | bytes 1572872 | tf_op jit(solution)/shard_map/ppermute | solution.py:32
  70.4 14.3 %collective-permute-start.15 = (bf16[512,512]{1,0:T(8,128)(2,1)S(1)}, bf16[512,512]{1,0:T(8,128)(2,1)S(1)}, u32[]{:S(2)}, u32[]{:S(2)}) collective-permute-start(bf16[512,512]{1,0:T(8,128)(2,1)S(1)} %copy-done.5), channel_id=1, source_target_pairs={{0,16},{8,24},{16,0},{24,8},{1,17},{9,25},{17,1},{25,9},{2,18},{10... | collective-permute-start | bytes 1572872 | tf_op jit(solution)/shard_map/ppermute | solution.py:32
  72.0 12.8 %collective-permute-start.14 = (bf16[512,512]{1,0:T(8,128)(2,1)S(1)}, bf16[512,512]{1,0:T(8,128)(2,1)S(1)}, u32[]{:S(2)}, u32[]{:S(2)}) collective-permute-start(bf16[512,512]{1,0:T(8,128)(2,1)S(1)} %copy-done.6), channel_id=1, source_target_pairs={{0,8},{8,0},{16,24},{24,16},{1,9},{9,1},{17,25},{25,17},{2,10},{10... | collective-permute-start | bytes 1572872 | tf_op jit(solution)/shard_map/ppermute | solution.py:32
  72.1 19.4 %collective-permute-start.17 = (bf16[512,512]{1,0:T(8,128)(2,1)S(1)}, bf16[512,512]{1,0:T(8,128)(2,1)S(1)}, u32[]{:S(2)}, u32[]{:S(2)}) collective-permute-start(bf16[512,512]{1,0:T(8,128)(2,1)S(1)} %get-tuple-element.42.rest_0_), channel_id=1, source_target_pairs={{0,8},{8,0},{16,24},{24,16},{1,9},{9,1},{17,25},{25,17},{2,10},{10... | collective-permute-start | bytes 1572872 | tf_op jit(solution)/shard_map/ppermute | solution.py:32
  84.7 6.8 %slice-start = ((s8[8388608]{0:T(1024)(128)(4,1)}), s8[4194304]{0:T(1024)(128)(4,1)S(1)}, s32[]{:S(2)}) async-start(s8[8388608]{0:T(1024)(128)(4,1)} %bitcast.57), calls=%async_computation | async-start | bytes 8388608
  85.6 6.0 %slice-start.1 = ((s8[8388608]{0:T(1024)(128)(4,1)}), s8[4194304]{0:T(1024)(128)(4,1)S(1)}, s32[]{:S(2)}) async-start(s8[8388608]{0:T(1024)(128)(4,1)} %bitcast.57), calls=%async_computation.1 | async-start | bytes 8388608
  86.7 4.8 %collective-permute-start.18 = (bf16[512,512]{1,0:T(8,128)(2,1)S(1)}, bf16[512,512]{1,0:T(8,128)(2,1)S(1)}, u32[]{:S(2)}, u32[]{:S(2)}) collective-permute-start(bf16[512,512]{1,0:T(8,128)(2,1)S(1)} %get-tuple-element.44.rest_1_), channel_id=1, source_target_pairs={{0,8},{8,0},{16,24},{24,16},{1,9},{9,1},{17,25},{25,17},{2,10},{10... | collective-permute-start | bytes 1572872 | tf_op jit(solution)/shard_map/ppermute | solution.py:32
  86.9 14.8 %collective-permute-start.11 = (bf16[512,512]{1,0:T(8,128)(2,1)S(1)}, bf16[512,512]{1,0:T(8,128)(2,1)S(1)}, u32[]{:S(2)}, u32[]{:S(2)}) collective-permute-start(bf16[512,512]{1,0:T(8,128)(2,1)S(1)} %get-tuple-element.42.rest_0_), channel_id=1, source_target_pairs={{0,16},{8,24},{16,0},{24,8},{1,17},{9,25},{17,1},{25,9},{2,18},{10... | collective-permute-start | bytes 1572872 | tf_op jit(solution)/shard_map/ppermute | solution.py:32
  88.4 24.1 %collective-permute-start.16 = (bf16[512,512]{1,0:T(8,128)(2,1)S(1)}, bf16[512,512]{1,0:T(8,128)(2,1)S(1)}, u32[]{:S(2)}, u32[]{:S(2)}) collective-permute-start(bf16[512,512]{1,0:T(8,128)(2,1)S(1)} %get-tuple-element.44.rest_1_), channel_id=1, source_target_pairs={{0,16},{8,24},{16,0},{24,8},{1,17},{9,25},{17,1},{25,9},{2,18},{10... | collective-permute-start | bytes 1572872 | tf_op jit(solution)/shard_map/ppermute | solution.py:32
  88.9 3.7 %copy-start.1 = (bf16[2048,1024]{1,0:T(8,128)(2,1)S(1)}, bf16[2048,1024]{1,0:T(8,128)(2,1)}, u32[]{:S(2)}) copy-start(bf16[2048,1024]{1,0:T(8,128)(2,1)} %basis.3) | copy-start | bytes 12582916
  112.4 1.9 %collective-permute-start.19 = (bf16[512,512]{1,0:T(8,128)(2,1)S(1)}, bf16[512,512]{1,0:T(8,128)(2,1)S(1)}, u32[]{:S(2)}, u32[]{:S(2)}) collective-permute-start(bf16[512,512]{1,0:T(8,128)(2,1)S(1)} %collective-permute-done.11.rest_0_), channel_id=1, source_target_pairs={{0,8},{8,0},{16,24},{24,16},{1,9},{9,1},{17,25},{25,17},{2,10},{10... | collective-permute-start | bytes 1572872 | tf_op jit(solution)/shard_map/ppermute | solution.py:32
  112.4 2.7 %collective-permute-start.20 = (bf16[512,512]{1,0:T(8,128)(2,1)S(1)}, bf16[512,512]{1,0:T(8,128)(2,1)S(1)}, u32[]{:S(2)}, u32[]{:S(2)}) collective-permute-start(bf16[512,512]{1,0:T(8,128)(2,1)S(1)} %collective-permute-done.16.rest_1_), channel_id=1, source_target_pairs={{0,8},{8,0},{16,24},{24,16},{1,9},{9,1},{17,25},{25,17},{2,10},{10... | collective-permute-start | bytes 1572872 | tf_op jit(solution)/shard_map/ppermute | solution.py:32
